TPU v7x, 32 devices: a whole 2x2x4 slice. The times are simulated.
32 devices in a mesh: dp: 8 (over z, x), mp: 4 (over y, core).
Axes of the slice: x: 2, y: 2, z: 4, core: 2. Of those that a mesh axis runs over, the one named last changes fastest.
Arguments:
- inputs: float32 [8, 1024, 768], P('dp', None, 'mp'), may hold values from -6 to 6
- lengths: int32 [8], P('dp'), may hold values from 64 to 1024, as said below
- ln1_gain: float32 [768], P('mp'), may hold values from 0.5 to 1.5
- ln1_bias: float32 [768], P('mp'), may hold values from -3 to 3
- w_query: float32 [768, 768], P(None, 'mp'), may hold values from -0.21875 to 0.21875
- w_key: float32 [768, 768], P(None, 'mp'), may hold values from -0.21875 to 0.21875
- w_value: float32 [768, 768], P(None, 'mp'), may hold values from -0.21875 to 0.21875
- query_bias: float32 [768], P('mp'), may hold values from -3 to 3
- value_bias: float32 [768], P('mp'), may hold values from -3 to 3
- pair_bias: float32 [1024, 256], replicated, may hold values from -3 to 3
- w_out: float32 [768, 768], P('mp'), may hold values from -0.875 to 0.875
- out_bias: float32 [768], P('mp'), may hold values from -3 to 3
- ln2_gain: float32 [768], P('mp'), may hold values from 0.5 to 1.5
- ln2_bias: float32 [768], P('mp'), may hold values from -3 to 3
- w_up: float32 [768, 3072], P(None, 'mp'), may hold values from -0.21875 to 0.21875
- up_bias: float32 [3072], P('mp'), may hold values from -3 to 3
- w_down: float32 [3072, 768], P('mp'), may hold values from -0.109375 to 0.109375
- down_bias: float32 [768], P('mp'), may hold values from -3 to 3
- cotangent: float32 [8, 1024, 768], P('dp', None, 'mp'), may hold values from -6 to 6
Outputs:
- result: float32 [8, 1024, 768], P('dp', None, 'mp')
- d_inputs: float32 [8, 1024, 768], P('dp', None, 'mp')
- d_ln1_gain: float32 [768], P('mp')
- d_ln1_bias: float32 [768], P('mp')
- d_w_query: float32 [768, 768], P(None, 'mp')
- d_w_key: float32 [768, 768], P(None, 'mp')
- d_w_value: float32 [768, 768], P(None, 'mp')
- d_query_bias: float32 [768], P('mp')
- d_value_bias: float32 [768], P('mp')
- d_pair_bias: float32 [1024, 256], replicated
- d_w_out: float32 [768, 768], P('mp')
- d_out_bias: float32 [768], P('mp')
- d_ln2_gain: float32 [768], P('mp')
- d_ln2_bias: float32 [768], P('mp')
- d_w_up: float32 [768, 3072], P(None, 'mp')
- d_up_bias: float32 [3072], P('mp')
- d_w_down: float32 [3072, 768], P('mp')
- d_down_bias: float32 [768], P('mp')
Inputs may be any that keep to these rules, and one draw needn't show every extreme that they name: `lengths`: some row of every draw has exactly 1024 live positions.
All inputs are finite; a program needn't handle non-finite values.
Results may differ from a plain program's by a relative error of at most 0.0003.
Values sent between devices are 32-bit elements; how exact they have to be, the bound alone decides.
No kernel may reach another device: no remote copies, remote signals or barrier semaphores. Data moves between devices by JAX's collectives and lax.ppermute only.
A program may use at most 192 MiB of HBM per device.

v0:
```python
import jax
import jax.numpy as jnp
from jax import lax
from jax.sharding import PartitionSpec as P

MODE = lax.Precision.HIGH
EPSILON = 1e-05


def dot_nn(left_arr, right_arr):
    return lax.dot_general(
        left_arr,
        right_arr,
        (((1,), (0,)), ((), ())),
        precision=MODE,
        preferred_element_type=jnp.float32,
    )


def dot_nt(left_arr, right_arr):
    return lax.dot_general(
        left_arr,
        right_arr,
        (((1,), (1,)), ((), ())),
        precision=MODE,
        preferred_element_type=jnp.float32,
    )


def dot_tn(left_arr, right_arr):
    return lax.dot_general(
        left_arr,
        right_arr,
        (((0,), (0,)), ((), ())),
        precision=MODE,
        preferred_element_type=jnp.float32,
    )


def swap(block, bit):
    return lax.ppermute(block, "mp", [(i, i ^ bit) for i in range(4)])


def gather_rows(own):
    rows, width = own.shape
    place = lax.axis_index("mp")
    far = swap(own, 2)
    near = swap(own, 1)
    far_near = swap(far, 1)
    whole = jnp.zeros((4 * rows, width), own.dtype)
    for flip, part in enumerate((own, near, far, far_near)):
        whole = lax.dynamic_update_slice(whole, part, ((place ^ flip) * rows, 0))
    return whole


def halve(grid, axis, bit):
    mine = lax.dynamic_index_in_dim(grid, bit, axis, keepdims=False)
    other = lax.dynamic_index_in_dim(grid, 1 - bit, axis, keepdims=False)
    return (mine, other)


def reduce_core(terms):
    rows, width = (terms.shape[0] // 4, terms.shape[1])
    place = lax.axis_index("mp")
    mine, other = halve(terms.reshape(2, 2, rows, width), 1, place & 1)
    return mine + swap(other, 1)


def scatter_sum(terms):
    place = lax.axis_index("mp")
    mine, other = halve(reduce_core(terms), 0, place >> 1)
    return mine + swap(other, 2)


def whole_sum(terms):
    place = lax.axis_index("mp")
    half = reduce_core(terms)
    half = half + swap(half, 2)
    other = swap(half, 1)
    odd = place & 1 == 1
    both = jnp.stack([jnp.where(odd, other, half), jnp.where(odd, half, other)], axis=1)
    return both.reshape(terms.shape)


def column_norm(values_in):
    mean = jnp.mean(values_in, axis=0, keepdims=True)
    var = jnp.mean(values_in * values_in, axis=0, keepdims=True) - mean * mean
    scale = lax.rsqrt(var + EPSILON)
    return ((values_in - mean) * scale, scale)


def band_blocks(pair_exp):
    span, window = pair_exp.shape
    count = span // window
    flipped = pair_exp.reshape(count, window, window)[:, :, ::-1]
    wide = jnp.pad(flipped, ((0, 0), (0, 0), (1, window)))
    skewed = wide.reshape(count, -1)[:, : window * 2 * window].reshape(count, window, 2 * window)
    query = jnp.arange(window, dtype=jnp.int32)[:, None]
    key = jnp.arange(2 * window, dtype=jnp.int32)[None, :]
    return skewed + (key <= query).astype(jnp.float32)[None]


def band_values(grid):
    window, wide = grid.shape
    flat = jnp.pad(grid.reshape(-1), (0, window))
    return flat.reshape(window, wide + 1)[:, 1 : window + 1][:, ::-1]


def body(
    inputs,
    lengths,
    ln1_gain,
    ln1_bias,
    w_query,
    w_key,
    w_value,
    query_bias,
    value_bias,
    pair_bias,
    w_out,
    out_bias,
    ln2_gain,
    ln2_bias,
    w_up,
    up_bias,
    w_down,
    down_bias,
    cotangent,
):
    seq_rows, span, chans = inputs.shape
    assert seq_rows == 1
    window = pair_bias.shape[1]
    count = span // window
    model = 4 * chans
    place = lax.axis_index("mp")
    live = (jnp.arange(span, dtype=jnp.int32) < lengths[0]).astype(jnp.float32)[None, :]

    def own_rows(whole):
        return lax.dynamic_slice_in_dim(whole, place * chans, chans, 0)

    x_own = inputs[0].T
    cot_own = cotangent[0].T
    vectors = jnp.stack([ln1_gain, ln1_bias, out_bias, ln2_gain, ln2_bias], axis=1)
    vectors = jnp.pad(vectors, ((0, 0), (0, 128 - vectors.shape[1])))
    gathered = gather_rows(jnp.concatenate([x_own, vectors], axis=1))
    whole_x = gathered[:, :span]
    gain_one, bias_one, bias_out, gain_two, bias_two = (
        gathered[:, span + i : span + i + 1] for i in range(5)
    )
    pair_exp = jnp.exp(pair_bias)
    bands = band_blocks(pair_exp)
    normal_one, scale_one = column_norm(whole_x)
    normed1 = normal_one * gain_one + bias_one
    w_qkv = jnp.concatenate([w_query.T, w_key.T, w_value.T], axis=0)
    projected = dot_nn(w_qkv, normed1)
    queries = projected[:chans] + query_bias[:, None]
    exp_keys = jnp.exp(projected[chans : 2 * chans])
    values = projected[2 * chans :] + value_bias[:, None]
    pair = jnp.concatenate([exp_keys * values, exp_keys], axis=0)
    sums = []
    far = jnp.zeros((2 * chans, 1), jnp.float32)
    for i in range(count):
        here = slice(i * window, (i + 1) * window)
        if i == 0:
            sums.append(dot_nt(pair[:, here], bands[i, :, window:]))
        else:
            near = pair[:, (i - 1) * window : (i + 1) * window]
            sums.append(dot_nt(near, bands[i]) + far)
            far = far + jnp.sum(pair[:, (i - 1) * window : i * window], axis=1, keepdims=True)
    sums = jnp.concatenate(sums, axis=1)
    denominator = sums[chans:]
    quotient = sums[:chans] / denominator
    gate_open = jax.nn.sigmoid(queries)
    mixed = gate_open * quotient
    w_out_whole = gather_rows(w_out)
    whole_cot = gather_rows(cot_own)
    mixed_whole = gather_rows(mixed)
    inner = whole_x + live * (dot_tn(w_out_whole, mixed_whole) + bias_out)
    normal_two, scale_two = column_norm(inner)
    normed2 = normal_two * gain_two + bias_two
    hidden_pre = dot_tn(w_up, normed2) + up_bias[:, None]
    hidden_act, gate_pull = jax.vjp(lambda v: jax.nn.gelu(v, approximate=True), hidden_pre)
    branch_two = live * whole_cot
    d_w_down = dot_nt(hidden_act, branch_two)
    (d_pre,) = gate_pull(dot_nn(w_down, branch_two))
    d_w_up = dot_nt(normed2, d_pre)
    d_up_bias = jnp.sum(d_pre, axis=1)
    d_down_bias = jnp.sum(live * cot_own, axis=1)
    d_normed2 = whole_sum(dot_nn(w_up, d_pre))
    ffn_grads = lax.psum((d_w_down, d_w_up), "dp")
    down_own = scatter_sum(dot_tn(w_down, hidden_act))
    result = own_rows(inner) + live * (down_own + down_bias[:, None])
    scaled_two = d_normed2 * gain_two
    d_inner = whole_cot + scale_two * (
        scaled_two
        - jnp.mean(scaled_two, axis=0, keepdims=True)
        - normal_two * jnp.mean(scaled_two * normal_two, axis=0, keepdims=True)
    )
    d_gain_two = jnp.sum(own_rows(d_normed2) * own_rows(normal_two), axis=1)
    d_bias_two = jnp.sum(own_rows(d_normed2), axis=1)
    branch_one = live * d_inner
    d_out_bias = jnp.sum(own_rows(branch_one), axis=1)
    d_w_out = dot_nt(mixed, branch_one)
    d_mixed = dot_nn(w_out, branch_one)
    d_queries = d_mixed * quotient * gate_open * (1.0 - gate_open)
    d_numer = d_mixed * gate_open / denominator
    d_pairs = jnp.concatenate([d_numer, -d_numer * quotient], axis=0)
    back = [None] * count
    d_bands = [None] * count
    later = jnp.zeros((2 * chans, 1), jnp.float32)
    for i in reversed(range(count)):
        here = slice(i * window, (i + 1) * window)
        before = slice(max(i - 1, 0) * window, (i + 1) * window)
        band = bands[i] if i else bands[i, :, window:]
        into = dot_nn(d_pairs[:, here], band)
        grid = dot_tn(d_pairs[:, here], pair[:, before])
        if i == 0:
            grid = jnp.pad(grid, ((0, 0), (window, 0)))
        d_bands[i] = band_values(grid)
        own_part = into[:, -window:] + later
        back[i] = own_part if back[i] is None else back[i] + own_part
        if i:
            back[i - 1] = into[:, :window]
            if i + 1 < count:
                ahead = slice((i + 1) * window, (i + 2) * window)
                later = later + jnp.sum(d_pairs[:, ahead], axis=1, keepdims=True)
    back = jnp.concatenate(back, axis=1)
    d_pair_bias = jnp.concatenate(d_bands, axis=0) * pair_exp
    d_values = exp_keys * back[:chans]
    d_keys = exp_keys * (values * back[:chans] + back[chans:])
    d_qkv = jnp.concatenate([d_queries, d_keys, d_values], axis=0)
    d_w_qkv = dot_nt(d_qkv, normed1)
    terms = dot_tn(w_qkv, d_qkv)
    scaled_terms = terms * gain_one
    stats = jnp.concatenate(
        [
            jnp.sum(scaled_terms, axis=0, keepdims=True),
            jnp.sum(scaled_terms * normal_one, axis=0, keepdims=True),
        ],
        axis=0,
    )
    stats = jnp.pad(stats, ((0, 6), (0, 0)))
    stats = stats + swap(stats, 1)
    stats = (stats + swap(stats, 2)) / model
    d_normed1 = scatter_sum(terms)
    normal_own = own_rows(normal_one)
    d_gain_one = jnp.sum(d_normed1 * normal_own, axis=1)
    d_bias_one = jnp.sum(d_normed1, axis=1)
    d_inputs = own_rows(d_inner) + scale_one * (
        d_normed1 * own_rows(gain_one) - stats[0:1] - normal_own * stats[1:2]
    )
    small = jnp.concatenate(
        [
            d_gain_one,
            d_bias_one,
            jnp.sum(d_queries, axis=1),
            jnp.sum(d_values, axis=1),
            d_out_bias,
            d_gain_two,
            d_bias_two,
            d_down_bias,
            d_up_bias,
        ]
    )
    d_w_qkv, d_w_out, small = lax.psum((d_w_qkv, d_w_out, small), "dp")
    d_pair_bias = lax.psum(d_pair_bias, ("dp", "mp"))
    vecs = [small[i * chans : (i + 1) * chans] for i in range(8)]
    return (
        result.T[None],
        d_inputs.T[None],
        vecs[0],
        vecs[1],
        d_w_qkv[:chans].T,
        d_w_qkv[chans : 2 * chans].T,
        d_w_qkv[2 * chans :].T,
        vecs[2],
        vecs[3],
        d_pair_bias,
        d_w_out,
        vecs[4],
        vecs[5],
        vecs[6],
        ffn_grads[1],
        small[8 * chans :],
        ffn_grads[0],
        vecs[7],
    )


def solution(mesh):
    rows = P("dp", None, "mp")
    vec = P("mp")
    out_dim = P(None, "mp")
    in_dim = P("mp", None)
    return jax.shard_map(
        body,
        mesh=mesh,
        in_specs=(
            rows,
            P("dp"),
            vec,
            vec,
            out_dim,
            out_dim,
            out_dim,
            vec,
            vec,
            P(),
            in_dim,
            vec,
            vec,
            vec,
            out_dim,
            vec,
            in_dim,
            vec,
            rows,
        ),
        out_specs=(
            rows,
            rows,
            vec,
            vec,
            out_dim,
            out_dim,
            out_dim,
            vec,
            vec,
            P(),
            in_dim,
            vec,
            vec,
            vec,
            out_dim,
            vec,
            in_dim,
            vec,
        ),
        check_vma=False,
    )
```

profile of v0, /device:TPU:0, one launch (start us, length us, event | category | flops | bytes accessed | tf_op | source)
XLA Modules:
  0.0 684.1 jit_solution(1836574850174201471)
XLA Ops:
  11.7 3.0 collective-permute-start.1
  14.7 20.0 %collective-permute-done.1 = f32[192,1152]{1,0:T(8,128)} collective-permute-done((f32[192,1152]{1,0:T(8,128)}, f32[192,1152]{1,0:T(8,128)}, u32[]{:S(2)}, u32[]{:S(2)}) %collective-permute-start.1) | collective-permute-done | bytes 884768 | tf_op jit(solution)/shard_map/ppermute | solution.py:41
  37.1 9.3 %rev.15 = f32[4,256,256]{2,1,0:T(8,128)} reverse(f32[4,256,256]{2,1,0:T(8,128)} %bitcast.164), dimensions={2} | reverse | bytes 2097152 | tf_op jit(solution)/shard_map/rev | solution.py:95
  46.4 3.2 pad.30
  49.6 5.6 reshape.167
  55.2 3.0 slice.228
  60.6 2.9 constant_dynamic-update-slice_fusion.14
  70.0 3.3 slice_reduce_fusion.2
  75.9 3.2 fusion.14
  87.8 30.4 %collective-permute-done.4 = f32[192,768]{1,0:T(8,128)} collective-permute-done((f32[192,768]{1,0:T(8,128)}, f32[192,768]{1,0:T(8,128)}, u32[]{:S(2)}, u32[]{:S(2)}) %collective-permute-start.4) | collective-permute-done | bytes 589856 | tf_op jit(solution)/shard_map/ppermute | solution.py:41
  128.0 6.3 fusion.88
  137.5 5.1 fusion.16
  142.7 4.7 fusion.31
  160.1 11.0 %collective-permute-done.12 = f32[192,1024]{1,0:T(8,128)} collective-permute-done((f32[192,1024]{1,0:T(8,128)}, f32[192,1024]{1,0:T(8,128)}, u32[]{:S(2)}, u32[]{:S(2)}) %collective-permute-start.12) | collective-permute-done | bytes 786464 | tf_op jit(solution)/shard_map/ppermute | solution.py:41
  171.1 16.4 %collective-permute-done.10 = f32[192,1024]{1,0:T(8,128)} collective-permute-done((f32[192,1024]{1,0:T(8,128)}, f32[192,1024]{1,0:T(8,128)}, u32[]{:S(2)}, u32[]{:S(2)}) %collective-permute-start.10) | collective-permute-done | bytes 786464 | tf_op jit(solution)/shard_map/ppermute | solution.py:41
  187.9 3.4 multiply_reduce_fusion.6
  195.1 10.2 %fusion.100 = (f32[768]{0:T(1024)}, f32[768,1024]{0,1:T(8,128)S(1)}) fusion(f32[1024,768]{1,0:T(8,128)S(1)} %copy-done.56, f32[768]{0:T(1024)S(1)} %copy-done.53, f32[768,768]{1,0:T(8,128)S(1)} %copy-done, f32[768,1024]{1,0:T(8,128)S(1)} %constant_dynamic-update-slice_fusion, f32[1024]{0:T(1024)S(1)} %fusion.63), kind=kOutput, calls=%fused_computation.206 | convolution fusion | flops 3641179392 | bytes 11806720 | tf_op jit(solution)/shard_map/dot_general | solution.py:11
  205.3 3.9 fusion.101
  209.4 3.4 collective-permute-done.14
  214.9 34.7 %collective-permute-done.15 = f32[2,192,1024]{2,1,0:T(8,128)S(1)} collective-permute-done((f32[2,192,1024]{2,1,0:T(8,128)S(1)}, f32[2,192,1024]{2,1,0:T(8,128)S(1)}, u32[]{:S(2)}, u32[]{:S(2)}) %collective-permute-start.15) | collective-permute-done | bytes 1572896 | tf_op jit(solution)/shard_map/ppermute | solution.py:41
  251.1 8.4 %fusion.15 = f32[768,768]{1,0:T(8,128)} fusion(f32[768,1024]{0,1:T(8,128)} %copy-done.31, f32[768,1024]{1,0:T(8,128)} %copy-done.24, f32[768]{0:T(1024)S(1)} %get-tuple-element.20, f32[768]{0:T(1024)S(1)} %get-tuple-element.18), kind=kOutput, calls=%fused_computation.33 | convolution fusion | flops 3625451520 | bytes 8656896 | tf_op jit(solution)/shard_map/dot_general | solution.py:21
  259.5 9.7 %fusion.9 = f32[768,768]{1,0:T(8,128)} fusion(f32[768,1024]{1,0:T(8,128)S(1)} %copy-done.16, f32[1024]{0:T(1024)S(1)} %fusion.63, f32[1024,768]{1,0:T(8,128)S(1)} %copy-done.57, f32[768]{0:T(1024)S(1)} %copy-done.53), kind=kOutput, calls=%fused_computation.27 | convolution fusion | flops 3631742976 | bytes 8657920 | tf_op jit(solution)/shard_map/dot_general | solution.py:21
  278.0 4.5 fusion.102
  282.5 3.4 fusion.91
  291.0 4.4 fusion.13
  295.5 7.2 %multiply_reduce_fusion.5 = (f32[1024]{0:T(1024)S(1)}, f32[1024]{0:T(1024)S(1)}, f32[768,1024]{1,0:T(8,128)S(1)}) fusion(f32[768]{0:T(1024)S(1)} %get-tuple-element.19, f32[768,1024]{1,0:T(8,128)} %copy-done.7, f32[192,1024]{1,0:T(8,128)S(1)} %get-tuple-element.38, f32[192,1024]{1,0:T(8,128)} %copy-done.40, f32[192,1024]{1,0:T(8,128)} %copy-done.54, ...), kind=kOutput, calls=%fused_computation.26 | convolution fusion | flops 2723117056 | bytes 10431488 | tf_op jit(solution)/shard_map/dot_general | solution.py:31
  311.3 3.3 rev.16
  335.3 14.7 %collective-permute-done.20 = f32[8,1024]{1,0:T(8,128)S(1)} collective-permute-done((f32[8,1024]{1,0:T(8,128)S(1)}, f32[8,1024]{1,0:T(8,128)S(1)}, u32[]{:S(2)}, u32[]{:S(2)}) %collective-permute-start.20) | collective-permute-done | bytes 32800 | tf_op jit(solution)/shard_map/ppermute | solution.py:41
  354.1 39.3 %psum.42 = f32[2304]{0:T(1024)S(1)} all-reduce(f32[2304]{0:T(1024)S(1)} %concatenate.38), channel_id=1, replica_groups=mesh['dp'=8,'mp'=4] {'dp'}, use_global_device_ids=true, to_apply=%region_21.22 | all-reduce | flops 2304 | bytes 18432 | tf_op jit(solution)/shard_map/psum | solution.py:265
  394.6 138.9 %all-reduce.14.cloned.1.call-done = (f32[576,768]{1,0:T(8,128)}, f32[192,768]{1,0:T(8,128)}, f32[768,768]{1,0:T(8,128)}, f32[768,768]{1,0:T(8,128)}) async-done(((f32[576,768]{1,0:T(8,128)}, f32[192,768]{1,0:T(8,128)}, f32[768,768]{1,0:T(8,128)}, f32[768,768]{1,0:T(8,128)}), (f32[576,768]{1,0:T(8,128)}, f32[192,768]{1,0:T(8,128)}, f32[768,768]{1,0:T(8,128)}, ...) | async-done | bytes 7077904 | tf_op jit(solution)/shard_map/psum | solution.py:265
  536.2 132.7 %all-reduce.12.cloned.1.call-done = f32[1024,256]{1,0:T(8,128)} async-done(((f32[1024,256]{1,0:T(8,128)}), f32[1024,256]{1,0:T(8,128)}) %all-reduce.12.cloned.1.call-update) | async-done | bytes 1048592 | tf_op jit(solution)/shard_map/psum | solution.py:266
  672.0 3.4 copy.101
  (256 shorter events, 114.8 us)
Async XLA Ops:
  7.2 135.5 %copy-start = (f32[768,768]{1,0:T(8,128)S(1)}, f32[768,768]{1,0:T(8,128)}, u32[]{:S(2)}) copy-start(f32[768,768]{1,0:T(8,128)} %param.35) | copy-start | bytes 7077892
  7.2 526.3 %all-reduce.14.cloned.1.call-start = ((), (), s32[]{:S(2)}) async-start(), calls=%async_computation.1 | async-start | bytes 14155776 | tf_op jit(solution)/shard_map/psum | solution.py:265
  11.7 23.0 %collective-permute-start.1 = (f32[192,1152]{1,0:T(8,128)}, f32[192,1152]{1,0:T(8,128)}, u32[]{:S(2)}, u32[]{:S(2)}) collective-permute-start(f32[192,1152]{1,0:T(8,128)} %get-tuple-element.70), channel_id=1, source_target_pairs={{0,2},{1,3},{2,0},{3,1},{4,6},{5,7},{6,4},{7,5},{8,10},{9,11},{10,... | collective-permute-start | bytes 2654216 | tf_op jit(solution)/shard_map/ppermute | solution.py:41
  14.7 45.9 %collective-permute-start = (f32[192,1152]{1,0:T(8,128)}, f32[192,1152]{1,0:T(8,128)}, u32[]{:S(2)}, u32[]{:S(2)}) collective-permute-start(f32[192,1152]{1,0:T(8,128)} %get-tuple-element.70), channel_id=1, source_target_pairs={{0,1},{1,0},{2,3},{3,2},{4,5},{5,4},{6,7},{7,6},{8,9},{9,8},{10,11... | collective-permute-start | bytes 2654216 | tf_op jit(solution)/shard_map/ppermute | solution.py:41
  34.7 30.9 %collective-permute-start.2 = (f32[192,1152]{1,0:T(8,128)}, f32[192,1152]{1,0:T(8,128)}, u32[]{:S(2)}, u32[]{:S(2)}) collective-permute-start(f32[192,1152]{1,0:T(8,128)} %collective-permute-done.1), channel_id=1, source_target_pairs={{0,1},{1,0},{2,3},{3,2},{4,5},{5,4},{6,7},{7,6},{8,9},{9,8},{10,11... | collective-permute-start | bytes 2654216 | tf_op jit(solution)/shard_map/ppermute | solution.py:41
  60.6 20.6 %copy-start.13 = (f32[4,256,512]{2,1,0:T(8,128)}, f32[4,256,512]{2,1,0:T(8,128)S(1)}, u32[]{:S(2)}) copy-start(f32[4,256,512]{2,1,0:T(8,128)S(1)} %bitcast_add_fusion) | copy-start | bytes 6291460
  85.2 33.6 %collective-permute-start.7 = (f32[192,1024]{1,0:T(8,128)}, f32[192,1024]{1,0:T(8,128)}, u32[]{:S(2)}, u32[]{:S(2)}) collective-permute-start(f32[192,1024]{1,0:T(8,128)} %get-tuple-element.51), channel_id=1, source_target_pairs={{0,2},{1,3},{2,0},{3,1},{4,6},{5,7},{6,4},{7,5},{8,10},{9,11},{10,... | collective-permute-start | bytes 2359304 | tf_op jit(solution)/shard_map/ppermute | solution.py:41
  87.0 31.2 %collective-permute-start.4 = (f32[192,768]{1,0:T(8,128)}, f32[192,768]{1,0:T(8,128)}, u32[]{:S(2)}, u32[]{:S(2)}) collective-permute-start(f32[192,768]{1,0:T(8,128)} %param.29), channel_id=1, source_target_pairs={{0,2},{1,3},{2,0},{3,1},{4,6},{5,7},{6,4},{7,5},{8,10},{9,11},{10,... | collective-permute-start | bytes 1769480 | tf_op jit(solution)/shard_map/ppermute | solution.py:41
  87.3 33.7 %collective-permute-start.3 = (f32[192,768]{1,0:T(8,128)}, f32[192,768]{1,0:T(8,128)}, u32[]{:S(2)}, u32[]{:S(2)}) collective-permute-start(f32[192,768]{1,0:T(8,128)} %param.29), channel_id=1, source_target_pairs={{0,1},{1,0},{2,3},{3,2},{4,5},{5,4},{6,7},{7,6},{8,9},{9,8},{10,11... | collective-permute-start | bytes 1769480 | tf_op jit(solution)/shard_map/ppermute | solution.py:41
  87.3 37.1 %collective-permute-start.6 = (f32[192,1024]{1,0:T(8,128)}, f32[192,1024]{1,0:T(8,128)}, u32[]{:S(2)}, u32[]{:S(2)}) collective-permute-start(f32[192,1024]{1,0:T(8,128)} %get-tuple-element.51), channel_id=1, source_target_pairs={{0,1},{1,0},{2,3},{3,2},{4,5},{5,4},{6,7},{7,6},{8,9},{9,8},{10,11... | collective-permute-start | bytes 2359304 | tf_op jit(solution)/shard_map/ppermute | solution.py:41
  118.1 5.1 collective-permute-start.5
  118.8 8.0 %collective-permute-start.8 = (f32[192,1024]{1,0:T(8,128)}, f32[192,1024]{1,0:T(8,128)}, u32[]{:S(2)}, u32[]{:S(2)}) collective-permute-start(f32[192,1024]{1,0:T(8,128)} %collective-permute-done.7), channel_id=1, source_target_pairs={{0,1},{1,0},{2,3},{3,2},{4,5},{5,4},{6,7},{7,6},{8,9},{9,8},{10,11... | collective-permute-start | bytes 2359304 | tf_op jit(solution)/shard_map/ppermute | solution.py:41
  150.4 3.8 collective-permute-start.9
  150.4 20.7 %collective-permute-start.12 = (f32[192,1024]{1,0:T(8,128)}, f32[192,1024]{1,0:T(8,128)}, u32[]{:S(2)}, u32[]{:S(2)}) collective-permute-start(f32[192,1024]{1,0:T(8,128)} %bitcast.27), channel_id=1, source_target_pairs={{0,2},{1,3},{2,0},{3,1},{4,6},{5,7},{6,4},{7,5},{8,10},{9,11},{10,... | collective-permute-start | bytes 2359304 | tf_op jit(solution)/shard_map/ppermute | solution.py:41
  157.4 30.5 %copy-start.52 = (f32[192]{0:T(256)S(1)}, f32[192]{0:T(256)}, u32[]{:S(2)}) copy-start(f32[192]{0:T(256)} %param.36) | copy-start | bytes 2308
  158.4 29.2 %collective-permute-start.10 = (f32[192,1024]{1,0:T(8,128)}, f32[192,1024]{1,0:T(8,128)}, u32[]{:S(2)}, u32[]{:S(2)}) collective-permute-start(f32[192,1024]{1,0:T(8,128)} %dynamic-slice_bitcast_fusion.4), channel_id=1, source_target_pairs={{0,2},{1,3},{2,0},{3,1},{4,6},{5,7},{6,4},{7,5},{8,10},{9,11},{10,... | collective-permute-start | bytes 2359304 | tf_op jit(solution)/shard_map/ppermute | solution.py:41
  160.1 31.2 %collective-permute-start.11 = (f32[192,1024]{1,0:T(8,128)}, f32[192,1024]{1,0:T(8,128)}, u32[]{:S(2)}, u32[]{:S(2)}) collective-permute-start(f32[192,1024]{1,0:T(8,128)} %bitcast.27), channel_id=1, source_target_pairs={{0,1},{1,0},{2,3},{3,2},{4,5},{5,4},{6,7},{7,6},{8,9},{9,8},{10,11... | collective-permute-start | bytes 2359304 | tf_op jit(solution)/shard_map/ppermute | solution.py:41
  171.1 22.8 %collective-permute-start.13 = (f32[192,1024]{1,0:T(8,128)}, f32[192,1024]{1,0:T(8,128)}, u32[]{:S(2)}, u32[]{:S(2)}) collective-permute-start(f32[192,1024]{1,0:T(8,128)} %collective-permute-done.12), channel_id=1, source_target_pairs={{0,1},{1,0},{2,3},{3,2},{4,5},{5,4},{6,7},{7,6},{8,9},{9,8},{10,11... | collective-permute-start | bytes 2359304 | tf_op jit(solution)/shard_map/ppermute | solution.py:41
  171.1 16.8 %copy-start.23 = (f32[2,192,1024]{2,1,0:T(8,128)S(1)}, f32[2,192,1024]{2,1,0:T(8,128)}, u32[]{:S(2)}) copy-start(f32[2,192,1024]{2,1,0:T(8,128)} %copy-done.22) | copy-start | bytes 4718596
  195.0 10.2 %copy-start.15 = (f32[768,1024]{1,0:T(8,128)}, f32[768,1024]{1,0:T(8,128)S(1)}, u32[]{:S(2)}) copy-start(f32[768,1024]{1,0:T(8,128)S(1)} %constant_dynamic-update-slice_fusion) | copy-start | bytes 9437188
  195.1 10.2 %copy-start.35 = (f32[768,768]{1,0:T(8,128)S(1)}, f32[768,768]{1,0:T(8,128)}, u32[]{:S(2)}) copy-start(f32[768,768]{1,0:T(8,128)} %param.33) | copy-start | bytes 7077892
  209.3 3.5 collective-permute-start.14
  213.1 36.5 %collective-permute-start.15 = (f32[2,192,1024]{2,1,0:T(8,128)S(1)}, f32[2,192,1024]{2,1,0:T(8,128)S(1)}, u32[]{:S(2)}, u32[]{:S(2)}) collective-permute-start(f32[2,192,1024]{2,1,0:T(8,128)S(1)} %bitcast_add_fusion.2), channel_id=1, source_target_pairs={{0,2},{1,3},{2,0},{3,1},{4,6},{5,7},{6,4},{7,5},{8,10},{9,11},{10,... | collective-permute-start | bytes 4718600 | tf_op jit(solution)/shard_map/ppermute | solution.py:41
  251.0 18.2 %collective-permute-start.16 = (f32[2,192,1024]{2,1,0:T(8,128)}, f32[2,192,1024]{2,1,0:T(8,128)}, u32[]{:S(2)}, u32[]{:S(2)}) collective-permute-start(f32[2,192,1024]{2,1,0:T(8,128)} %add.320), channel_id=1, source_target_pairs={{0,1},{1,0},{2,3},{3,2},{4,5},{5,4},{6,7},{7,6},{8,9},{9,8},{10,11... | collective-permute-start | bytes 4718600 | tf_op jit(solution)/shard_map/ppermute | solution.py:41
  295.4 373.5 %all-reduce.12.cloned.1.call-start = ((), (), s32[]{:S(2)}) async-start(), calls=%async_computation | async-start | bytes 2097152 | tf_op jit(solution)/shard_map/psum | solution.py:266
  304.0 20.7 %collective-permute-start.17 = (f32[2,192,1024]{2,1,0:T(8,128)}, f32[2,192,1024]{2,1,0:T(8,128)}, u32[]{:S(2)}, u32[]{:S(2)}) collective-permute-start(f32[2,192,1024]{2,1,0:T(8,128)} %dynamic-slice_bitcast_fusion), channel_id=1, source_target_pairs={{0,1},{1,0},{2,3},{3,2},{4,5},{5,4},{6,7},{7,6},{8,9},{9,8},{10,11... | collective-permute-start | bytes 4718600 | tf_op jit(solution)/shard_map/ppermute | solution.py:41
  305.5 9.1 %copy-start.5 = (f32[192,1024]{1,0:T(8,128)S(1)}, f32[192,1024]{1,0:T(8,128)}, u32[]{:S(2)}) copy-start(f32[192,1024]{1,0:T(8,128)} %copy-done.4) | copy-start | bytes 2359300
  324.5 7.6 %collective-permute-start.19 = (f32[8,1024]{1,0:T(8,128)S(1)}, f32[8,1024]{1,0:T(8,128)S(1)}, u32[]{:S(2)}, u32[]{:S(2)}) collective-permute-start(f32[8,1024]{1,0:T(8,128)S(1)} %select_maximum_fusion.1), channel_id=1, source_target_pairs={{0,1},{1,0},{2,3},{3,2},{4,5},{5,4},{6,7},{7,6},{8,9},{9,8},{10,11... | collective-permute-start | bytes 98312 | tf_op jit(solution)/shard_map/ppermute | solution.py:41
  329.2 20.9 %copy-start.9 = (f32[768,1024]{1,0:T(8,128)S(1)}, f32[768,1024]{1,0:T(8,128)}, u32[]{:S(2)}) copy-start(f32[768,1024]{1,0:T(8,128)} %copy-done.7) | copy-start | bytes 9437188
  329.2 20.9 %collective-permute-start.18 = (f32[192,1024]{1,0:T(8,128)}, f32[192,1024]{1,0:T(8,128)}, u32[]{:S(2)}, u32[]{:S(2)}) collective-permute-start(f32[192,1024]{1,0:T(8,128)} %dynamic-slice_bitcast_fusion.3), channel_id=1, source_target_pairs={{0,2},{1,3},{2,0},{3,1},{4,6},{5,7},{6,4},{7,5},{8,10},{9,11},{10,... | collective-permute-start | bytes 2359304 | tf_op jit(solution)/shard_map/ppermute | solution.py:41
  332.2 17.8 %collective-permute-start.20 = (f32[8,1024]{1,0:T(8,128)S(1)}, f32[8,1024]{1,0:T(8,128)S(1)}, u32[]{:S(2)}, u32[]{:S(2)}) collective-permute-start(f32[8,1024]{1,0:T(8,128)S(1)} %fusion.64), channel_id=1, source_target_pairs={{0,2},{1,3},{2,0},{3,1},{4,6},{5,7},{6,4},{7,5},{8,10},{9,11},{10,... | collective-permute-start | bytes 98312 | tf_op jit(solution)/shard_map/ppermute | solution.py:41
  533.5 137.7 %copy-start.41 = (f32[192,768]{1,0:T(8,128)S(1)}, f32[192,768]{1,0:T(8,128)}, u32[]{:S(2)}) copy-start(f32[192,768]{1,0:T(8,128)} %get-tuple-element.108) | copy-start | bytes 1769476
  (49 other events, 179.2 us)
Sparse Core Ops, SparseCore 0:
  295.6 237.8 all-reduce.13
  540.1 128.8 all-reduce.11
where the time goes:
time: 695 us; the launch traced here: 684 us
  waiting for transfers between devices  404 us (58%)
  local copies, waits for them, and re-layouts  96.8 us (14%)
  matrix products  77.3 us (11%)
  blocking collectives  39.3 us (6%)
  other arithmetic  35.8 us (5%)
  between operations  16.3 us (2%)
  starting transfers between devices  14.4 us (2%)
    psum x1, waiting for transfers between devices, body(): d_w_qkv, d_w_out, small = lax.psum((d_w_qkv, d_w_out, small), 'dp')  139 us
    psum x1, waiting for transfers between devices, body(): d_pair_bias = lax.psum(d_pair_bias, ('dp', 'mp'))  133 us
    ppermute x21, waiting for transfers between devices, swap(): return lax.ppermute(block, 'mp', [(i, i ^ bit) for i in range(4)])  133 us
    psum x1, blocking collectives, body(): d_w_qkv, d_w_out, small = lax.psum((d_w_qkv, d_w_out, small), 'dp')  39.3 us
    dot_general x8, matrix products, dot_nt(): lax.dot_general(left_arr, right_arr, (((1,), (1,)), ((), ())), precision=...  28.9 us
    dot_general x8, matrix products, dot_tn(): lax.dot_general(left_arr, right_arr, (((0,), (0,)), ((), ())), precision=...  25.8 us
    dot_general x8, matrix products, dot_nn(): lax.dot_general(left_arr, right_arr, (((1,), (0,)), ((), ())), precision=...  22.6 us
    unnamed x125, local copies, waits for them, and re-layouts  21.3 us
  transfers between devices with their start and end apart: 23, of which 11 were waited for; matrix products, arithmetic and copies ran while one was open for 16% of the time, Pallas kernels for 0%

commit v1 on v0

--- a/solution.py
+++ b/solution.py
@@ -263,7 +263,7 @@
         ]
     )
     d_w_qkv, d_w_out, small = lax.psum((d_w_qkv, d_w_out, small), "dp")
-    d_pair_bias = lax.psum(d_pair_bias, ("dp", "mp"))
+    d_pair_bias = lax.psum(lax.psum(d_pair_bias, "mp"), "dp")
     vecs = [small[i * chans : (i + 1) * chans] for i in range(8)]
     return (
         result.T[None],

time: 695 us -> 651 us (0.937)
  waiting for transfers between devices: 404 us -> 361 us
    psum x1, waiting for transfers between devices: 133 us -> 27.5 us  [body(): d_pair_bias = lax.psum(lax.psum(d_pair_bias, 'mp'), 'dp')]
    psum x1, waiting for transfers between devices: 139 us -> 198 us  [body(): d_w_qkv, d_w_out, small = lax.psum((d_w_qkv, d_w_out, small), 'dp')]
    unnamed x125 -> x141, local copies, waits for them, and re-layouts: 21.3 us -> 20.1 us
  transfers between devices with their start and end apart: 23 -> 23, of which waited for: 11 -> 12; matrix products, arithmetic and copies ran while one was open for 16% -> 14% of each run, Pallas kernels for 0% -> 0%
where the time goes in v1:
time: 651 us; the launch traced here: 640 us
  waiting for transfers between devices  361 us (55%)
  local copies, waits for them, and re-layouts  91.7 us (14%)
  matrix products  83.3 us (13%)
  blocking collectives  39.4 us (6%)
  other arithmetic  34.2 us (5%)
  between operations  16.2 us (2%)
  starting transfers between devices  14 us (2%)
    psum x1, waiting for transfers between devices, body(): d_w_qkv, d_w_out, small = lax.psum((d_w_qkv, d_w_out, small), 'dp')  198 us
    ppermute x21, waiting for transfers between devices, swap(): return lax.ppermute(block, 'mp', [(i, i ^ bit) for i in range(4)])  136 us
    psum x1, blocking collectives, body(): d_w_qkv, d_w_out, small = lax.psum((d_w_qkv, d_w_out, small), 'dp')  39.4 us
    dot_general x8, matrix products, dot_nt(): lax.dot_general(left_arr, right_arr, (((1,), (1,)), ((), ())), precision=...  28.8 us
    dot_general x8, matrix products, dot_tn(): lax.dot_general(left_arr, right_arr, (((0,), (0,)), ((), ())), precision=...  27.7 us
    psum x1, waiting for transfers between devices, body(): d_pair_bias = lax.psum(lax.psum(d_pair_bias, 'mp'), 'dp')  27.5 us
    dot_general x8, matrix products, dot_nn(): lax.dot_general(left_arr, right_arr, (((1,), (0,)), ((), ())), precision=...  26.8 us
    unnamed x141, local copies, waits for them, and re-layouts  20.1 us
  transfers between devices with their start and end apart: 23, of which 12 were waited for; matrix products, arithmetic and copies ran while one was open for 14% of the time, Pallas kernels for 0%

profile of v1, /device:TPU:0, one launch (start us, length us, event | category | flops | bytes accessed | tf_op | source)
XLA Modules:
  0.0 639.8 jit_solution(9315386483670460231)
XLA Ops:
  11.6 3.0 collective-permute-start.1
  14.7 20.0 %collective-permute-done.1 = f32[192,1152]{1,0:T(8,128)} collective-permute-done((f32[192,1152]{1,0:T(8,128)}, f32[192,1152]{1,0:T(8,128)}, u32[]{:S(2)}, u32[]{:S(2)}) %collective-permute-start.1) | collective-permute-done | bytes 884768 | tf_op jit(solution)/shard_map/ppermute | solution.py:41
  36.6 7.5 %rev.15 = f32[4,256,256]{2,1,0:T(8,128)S(1)} reverse(f32[4,256,256]{2,1,0:T(8,128)} %bitcast.164), dimensions={2} | reverse | bytes 2097152 | tf_op jit(solution)/shard_map/rev | solution.py:95
  46.2 5.6 reshape.167
  51.8 3.1 slice.228
  57.2 2.8 constant_dynamic-update-slice_fusion.14
  66.6 3.8 slice_reduce_fusion.2
  73.1 3.2 fusion.14
  84.9 30.4 %collective-permute-done.4 = f32[192,768]{1,0:T(8,128)} collective-permute-done((f32[192,768]{1,0:T(8,128)}, f32[192,768]{1,0:T(8,128)}, u32[]{:S(2)}, u32[]{:S(2)}) %collective-permute-start.4) | collective-permute-done | bytes 589856 | tf_op jit(solution)/shard_map/ppermute | solution.py:41
  125.2 6.3 fusion.88
  134.7 4.7 fusion.16
  139.4 4.7 fusion.31
  156.8 11.0 %collective-permute-done.12 = f32[192,1024]{1,0:T(8,128)} collective-permute-done((f32[192,1024]{1,0:T(8,128)}, f32[192,1024]{1,0:T(8,128)}, u32[]{:S(2)}, u32[]{:S(2)}) %collective-permute-start.12) | collective-permute-done | bytes 786464 | tf_op jit(solution)/shard_map/ppermute | solution.py:41
  167.8 16.4 %collective-permute-done.10 = f32[192,1024]{1,0:T(8,128)} collective-permute-done((f32[192,1024]{1,0:T(8,128)}, f32[192,1024]{1,0:T(8,128)}, u32[]{:S(2)}, u32[]{:S(2)}) %collective-permute-start.10) | collective-permute-done | bytes 786464 | tf_op jit(solution)/shard_map/ppermute | solution.py:41
  184.6 3.4 multiply_reduce_fusion.6
  191.7 10.2 %fusion.100 = (f32[768]{0:T(1024)}, f32[768,1024]{0,1:T(8,128)S(1)}) fusion(f32[1024,768]{1,0:T(8,128)S(1)} %copy-done.64, f32[768]{0:T(1024)S(1)} %copy-done.60, f32[768,768]{1,0:T(8,128)S(1)} %copy-done, f32[768,1024]{1,0:T(8,128)S(1)} %constant_dynamic-update-slice_fusion, f32[1024]{0:T(1024)S(1)} %fusion.63), kind=kOutput, calls=%fused_computation.206 | convolution fusion | flops 3641179392 | bytes 11806720 | tf_op jit(solution)/shard_map/dot_general | solution.py:11
  202.0 3.9 fusion.101
  206.1 3.4 collective-permute-done.14
  211.6 34.7 %collective-permute-done.15 = f32[2,192,1024]{2,1,0:T(8,128)S(1)} collective-permute-done((f32[2,192,1024]{2,1,0:T(8,128)S(1)}, f32[2,192,1024]{2,1,0:T(8,128)S(1)}, u32[]{:S(2)}, u32[]{:S(2)}) %collective-permute-start.15) | collective-permute-done | bytes 1572896 | tf_op jit(solution)/shard_map/ppermute | solution.py:41
  246.8 8.4 %fusion.15 = f32[768,768]{1,0:T(8,128)} fusion(f32[768,1024]{0,1:T(8,128)} %copy-done.25, f32[768,1024]{1,0:T(8,128)} %copy-done.22, f32[768]{0:T(1024)S(1)} %copy-done.51, f32[768]{0:T(1024)S(1)} %get-tuple-element.18), kind=kOutput, calls=%fused_computation.33 | convolution fusion | flops 3625451520 | bytes 8656896 | tf_op jit(solution)/shard_map/dot_general | solution.py:21
  255.2 9.7 %fusion.9 = f32[768,768]{1,0:T(8,128)} fusion(f32[768,1024]{1,0:T(8,128)S(1)} %copy-done.15, f32[1024]{0:T(1024)S(1)} %fusion.63, f32[1024,768]{1,0:T(8,128)S(1)} %copy-done.65, f32[768]{0:T(1024)S(1)} %copy-done.61), kind=kOutput, calls=%fused_computation.27 | convolution fusion | flops 3631742976 | bytes 8657920 | tf_op jit(solution)/shard_map/dot_general | solution.py:21
  270.2 2.8 broadcast_multiply_fusion
  273.0 4.5 fusion.102
  277.5 3.8 fusion.91
  319.0 4.4 fusion.13
  323.4 27.5 %all-reduce.12.cloned.1.call-done = f32[1024,256]{1,0:T(8,128)} async-done(((f32[1024,256]{1,0:T(8,128)}), f32[1024,256]{1,0:T(8,128)}) %all-reduce.12.cloned.1.call-update) | async-done | bytes 1048592 | tf_op jit(solution)/shard_map/psum | solution.py:266
  350.8 7.0 %multiply_reduce_fusion.5 = (f32[1024]{0:T(1024)S(1)}, f32[1024]{0:T(1024)S(1)}, f32[768,1024]{1,0:T(8,128)S(1)}) fusion(f32[768]{0:T(1024)S(1)} %copy-done.47, f32[768,1024]{1,0:T(8,128)S(1)} %copy-done.8, f32[192,1024]{1,0:T(8,128)} %copy-done.38, f32[192,1024]{1,0:T(8,128)} %copy-done.39, f32[192,1024]{1,0:T(8,128)} %get-tuple-element.41, ...), kind=kOutput, calls=%fused_computation.26 | convolution fusion | flops 2723117056 | bytes 10431488 | tf_op jit(solution)/shard_map/dot_general | solution.py:31
  358.1 3.4 collective-permute-done.17
  368.3 14.1 %collective-permute-done.20 = f32[8,1024]{1,0:T(8,128)S(1)} collective-permute-done((f32[8,1024]{1,0:T(8,128)S(1)}, f32[8,1024]{1,0:T(8,128)S(1)}, u32[]{:S(2)}, u32[]{:S(2)}) %collective-permute-start.20) | collective-permute-done | bytes 32800 | tf_op jit(solution)/shard_map/ppermute | solution.py:41
  383.5 39.4 %psum.49 = f32[2304]{0:T(1024)S(1)} all-reduce(f32[2304]{0:T(1024)S(1)} %concatenate.38), channel_id=1, replica_groups=mesh['dp'=8,'mp'=4] {'dp'}, use_global_device_ids=true, to_apply=%region_21.22 | all-reduce | flops 2304 | bytes 18432 | tf_op jit(solution)/shard_map/psum | solution.py:265
  426.7 197.9 %all-reduce.14.cloned.1.call-done = (f32[576,768]{1,0:T(8,128)}, f32[1024,256]{1,0:T(8,128)}, f32[192,768]{1,0:T(8,128)}, f32[768,768]{1,0:T(8,128)}, f32[768,768]{1,0:T(8,128)}) async-done(((f32[576,768]{1,0:T(8,128)}, f32[1024,256]{1,0:T(8,128)}, f32[192,768]{1,0:T(8,128)}, f32[768,768]{1,0:T(8,128)}, f32[768,768]{1,0:T(8,128)}), (f32[576,768]{1,0:T(8,128)}, f32[1024,256]{1,0:T(8,128)}, ...) | async-done | bytes 8126480 | tf_op jit(solution)/shard_map/psum | solution.py:265
  624.5 2.8 slice_bitcast_fusion
  (272 shorter events, 119.8 us)
Async XLA Ops:
  7.2 132.2 %copy-start = (f32[768,768]{1,0:T(8,128)S(1)}, f32[768,768]{1,0:T(8,128)}, u32[]{:S(2)}) copy-start(f32[768,768]{1,0:T(8,128)} %param.35) | copy-start | bytes 7077892
  7.2 343.6 %all-reduce.12.cloned.1.call-start = ((), (), s32[]{:S(2)}) async-start(), calls=%async_computation | async-start | bytes 2097152 | tf_op jit(solution)/shard_map/psum | solution.py:266
  8.3 27.2 %copy-start.23 = (f32[1024,256]{1,0:T(8,128)S(1)}, f32[1024,256]{1,0:T(8,128)}, u32[]{:S(2)}) copy-start(f32[1024,256]{1,0:T(8,128)} %param.28) | copy-start | bytes 3145732
  11.6 23.0 %collective-permute-start.1 = (f32[192,1152]{1,0:T(8,128)}, f32[192,1152]{1,0:T(8,128)}, u32[]{:S(2)}, u32[]{:S(2)}) collective-permute-start(f32[192,1152]{1,0:T(8,128)} %get-tuple-element.71), channel_id=1, source_target_pairs={{0,2},{1,3},{2,0},{3,1},{4,6},{5,7},{6,4},{7,5},{8,10},{9,11},{10,... | collective-permute-start | bytes 2654216 | tf_op jit(solution)/shard_map/ppermute | solution.py:41
  14.7 42.5 %collective-permute-start = (f32[192,1152]{1,0:T(8,128)}, f32[192,1152]{1,0:T(8,128)}, u32[]{:S(2)}, u32[]{:S(2)}) collective-permute-start(f32[192,1152]{1,0:T(8,128)} %get-tuple-element.71), channel_id=1, source_target_pairs={{0,1},{1,0},{2,3},{3,2},{4,5},{5,4},{6,7},{7,6},{8,9},{9,8},{10,11... | collective-permute-start | bytes 2654216 | tf_op jit(solution)/shard_map/ppermute | solution.py:41
  34.7 27.6 %collective-permute-start.2 = (f32[192,1152]{1,0:T(8,128)}, f32[192,1152]{1,0:T(8,128)}, u32[]{:S(2)}, u32[]{:S(2)}) collective-permute-start(f32[192,1152]{1,0:T(8,128)} %collective-permute-done.1), channel_id=1, source_target_pairs={{0,1},{1,0},{2,3},{3,2},{4,5},{5,4},{6,7},{7,6},{8,9},{9,8},{10,11... | collective-permute-start | bytes 2654216 | tf_op jit(solution)/shard_map/ppermute | solution.py:41
  57.2 21.1 %copy-start.12 = (f32[4,256,512]{2,1,0:T(8,128)}, f32[4,256,512]{2,1,0:T(8,128)S(1)}, u32[]{:S(2)}) copy-start(f32[4,256,512]{2,1,0:T(8,128)S(1)} %bitcast_add_fusion) | copy-start | bytes 6291460
  82.4 33.6 %collective-permute-start.7 = (f32[192,1024]{1,0:T(8,128)}, f32[192,1024]{1,0:T(8,128)}, u32[]{:S(2)}, u32[]{:S(2)}) collective-permute-start(f32[192,1024]{1,0:T(8,128)} %get-tuple-element.52), channel_id=1, source_target_pairs={{0,2},{1,3},{2,0},{3,1},{4,6},{5,7},{6,4},{7,5},{8,10},{9,11},{10,... | collective-permute-start | bytes 2359304 | tf_op jit(solution)/shard_map/ppermute | solution.py:41
  84.1 31.2 %collective-permute-start.4 = (f32[192,768]{1,0:T(8,128)}, f32[192,768]{1,0:T(8,128)}, u32[]{:S(2)}, u32[]{:S(2)}) collective-permute-start(f32[192,768]{1,0:T(8,128)} %param.29), channel_id=1, source_target_pairs={{0,2},{1,3},{2,0},{3,1},{4,6},{5,7},{6,4},{7,5},{8,10},{9,11},{10,... | collective-permute-start | bytes 1769480 | tf_op jit(solution)/shard_map/ppermute | solution.py:41
  84.4 33.8 %collective-permute-start.3 = (f32[192,768]{1,0:T(8,128)}, f32[192,768]{1,0:T(8,128)}, u32[]{:S(2)}, u32[]{:S(2)}) collective-permute-start(f32[192,768]{1,0:T(8,128)} %param.29), channel_id=1, source_target_pairs={{0,1},{1,0},{2,3},{3,2},{4,5},{5,4},{6,7},{7,6},{8,9},{9,8},{10,11... | collective-permute-start | bytes 1769480 | tf_op jit(solution)/shard_map/ppermute | solution.py:41
  84.4 37.1 %collective-permute-start.6 = (f32[192,1024]{1,0:T(8,128)}, f32[192,1024]{1,0:T(8,128)}, u32[]{:S(2)}, u32[]{:S(2)}) collective-permute-start(f32[192,1024]{1,0:T(8,128)} %get-tuple-element.52), channel_id=1, source_target_pairs={{0,1},{1,0},{2,3},{3,2},{4,5},{5,4},{6,7},{7,6},{8,9},{9,8},{10,11... | collective-permute-start | bytes 2359304 | tf_op jit(solution)/shard_map/ppermute | solution.py:41
  115.3 5.1 collective-permute-start.5
  116.0 8.0 %collective-permute-start.8 = (f32[192,1024]{1,0:T(8,128)}, f32[192,1024]{1,0:T(8,128)}, u32[]{:S(2)}, u32[]{:S(2)}) collective-permute-start(f32[192,1024]{1,0:T(8,128)} %collective-permute-done.7), channel_id=1, source_target_pairs={{0,1},{1,0},{2,3},{3,2},{4,5},{5,4},{6,7},{7,6},{8,9},{9,8},{10,11... | collective-permute-start | bytes 2359304 | tf_op jit(solution)/shard_map/ppermute | solution.py:41
  147.1 3.8 collective-permute-start.9
  147.1 20.7 %collective-permute-start.12 = (f32[192,1024]{1,0:T(8,128)}, f32[192,1024]{1,0:T(8,128)}, u32[]{:S(2)}, u32[]{:S(2)}) collective-permute-start(f32[192,1024]{1,0:T(8,128)} %bitcast.27), channel_id=1, source_target_pairs={{0,2},{1,3},{2,0},{3,1},{4,6},{5,7},{6,4},{7,5},{8,10},{9,11},{10,... | collective-permute-start | bytes 2359304 | tf_op jit(solution)/shard_map/ppermute | solution.py:41
  155.0 29.2 %collective-permute-start.10 = (f32[192,1024]{1,0:T(8,128)}, f32[192,1024]{1,0:T(8,128)}, u32[]{:S(2)}, u32[]{:S(2)}) collective-permute-start(f32[192,1024]{1,0:T(8,128)} %dynamic-slice_bitcast_fusion.4), channel_id=1, source_target_pairs={{0,2},{1,3},{2,0},{3,1},{4,6},{5,7},{6,4},{7,5},{8,10},{9,11},{10,... | collective-permute-start | bytes 2359304 | tf_op jit(solution)/shard_map/ppermute | solution.py:41
  156.8 31.2 %collective-permute-start.11 = (f32[192,1024]{1,0:T(8,128)}, f32[192,1024]{1,0:T(8,128)}, u32[]{:S(2)}, u32[]{:S(2)}) collective-permute-start(f32[192,1024]{1,0:T(8,128)} %bitcast.27), channel_id=1, source_target_pairs={{0,1},{1,0},{2,3},{3,2},{4,5},{5,4},{6,7},{7,6},{8,9},{9,8},{10,11... | collective-permute-start | bytes 2359304 | tf_op jit(solution)/shard_map/ppermute | solution.py:41
  167.7 22.8 %collective-permute-start.13 = (f32[192,1024]{1,0:T(8,128)}, f32[192,1024]{1,0:T(8,128)}, u32[]{:S(2)}, u32[]{:S(2)}) collective-permute-start(f32[192,1024]{1,0:T(8,128)} %collective-permute-done.12), channel_id=1, source_target_pairs={{0,1},{1,0},{2,3},{3,2},{4,5},{5,4},{6,7},{7,6},{8,9},{9,8},{10,11... | collective-permute-start | bytes 2359304 | tf_op jit(solution)/shard_map/ppermute | solution.py:41
  167.8 16.8 %copy-start.21 = (f32[2,192,1024]{2,1,0:T(8,128)S(1)}, f32[2,192,1024]{2,1,0:T(8,128)}, u32[]{:S(2)}) copy-start(f32[2,192,1024]{2,1,0:T(8,128)} %copy-done.20) | copy-start | bytes 4718596
  167.8 16.8 %copy-start.58 = (f32[192]{0:T(256)S(1)}, f32[192]{0:T(256)}, u32[]{:S(2)}) copy-start(f32[192]{0:T(256)} %param.36) | copy-start | bytes 2308
  206.0 3.5 collective-permute-start.14
  209.8 37.0 %copy-start.51 = (f32[768]{0:T(1024)S(1)}, f32[768]{0:T(1024)}, u32[]{:S(2)}) copy-start(f32[768]{0:T(1024)} %get-tuple-element.20) | copy-start | bytes 9220
  209.8 36.5 %collective-permute-start.15 = (f32[2,192,1024]{2,1,0:T(8,128)S(1)}, f32[2,192,1024]{2,1,0:T(8,128)S(1)}, u32[]{:S(2)}, u32[]{:S(2)}) collective-permute-start(f32[2,192,1024]{2,1,0:T(8,128)S(1)} %bitcast_add_fusion.2), channel_id=1, source_target_pairs={{0,2},{1,3},{2,0},{3,1},{4,6},{5,7},{6,4},{7,5},{8,10},{9,11},{10,... | collective-permute-start | bytes 4718600 | tf_op jit(solution)/shard_map/ppermute | solution.py:41
  246.6 18.3 %collective-permute-start.16 = (f32[2,192,1024]{2,1,0:T(8,128)S(1)}, f32[2,192,1024]{2,1,0:T(8,128)}, u32[]{:S(2)}, u32[]{:S(2)}) collective-permute-start(f32[2,192,1024]{2,1,0:T(8,128)S(1)} %add.322), channel_id=1, source_target_pairs={{0,1},{1,0},{2,3},{3,2},{4,5},{5,4},{6,7},{7,6},{8,9},{9,8},{10,11... | collective-permute-start | bytes 4718600 | tf_op jit(solution)/shard_map/ppermute | solution.py:41
  313.0 311.5 %all-reduce.14.cloned.1.call-start = ((), (), s32[]{:S(2)}) async-start(), calls=%async_computation.1 | async-start | bytes 16252928 | tf_op jit(solution)/shard_map/psum | solution.py:265
  358.0 3.5 collective-permute-start.17
  361.9 21.5 %copy-start.52 = (f32[768]{0:T(1024)S(1)}, f32[768]{0:T(1024)}, u32[]{:S(2)}) copy-start(f32[768]{0:T(1024)} %get-tuple-element.95) | copy-start | bytes 9220
  362.0 21.4 %copy-start.55 = (f32[192]{0:T(256)S(1)}, f32[192]{0:T(256)}, u32[]{:S(2)}) copy-start(f32[192]{0:T(256)} %get-tuple-element.73) | copy-start | bytes 2308
  362.0 62.2 %copy-start.45 = (f32[1024]{0:T(1024)S(1)}, f32[1024]{0:T(1024)}, u32[]{:S(2)}) copy-start(f32[1024]{0:T(1024)} %copy-done.44) | copy-start | bytes 12292
  362.0 20.4 %collective-permute-start.18 = (f32[192,1024]{1,0:T(8,128)S(1)}, f32[192,1024]{1,0:T(8,128)S(1)}, u32[]{:S(2)}, u32[]{:S(2)}) collective-permute-start(f32[192,1024]{1,0:T(8,128)S(1)} %dynamic-slice_bitcast_fusion.3), channel_id=1, source_target_pairs={{0,2},{1,3},{2,0},{3,1},{4,6},{5,7},{6,4},{7,5},{8,10},{9,11},{10,... | collective-permute-start | bytes 2359304 | tf_op jit(solution)/shard_map/ppermute | solution.py:41
  363.0 1.3 collective-permute-start.19
  364.3 18.0 %collective-permute-start.20 = (f32[8,1024]{1,0:T(8,128)S(1)}, f32[8,1024]{1,0:T(8,128)S(1)}, u32[]{:S(2)}, u32[]{:S(2)}) collective-permute-start(f32[8,1024]{1,0:T(8,128)S(1)} %fusion.64), channel_id=1, source_target_pairs={{0,2},{1,3},{2,0},{3,1},{4,6},{5,7},{6,4},{7,5},{8,10},{9,11},{10,... | collective-permute-start | bytes 98312 | tf_op jit(solution)/shard_map/ppermute | solution.py:41
  (57 other events, 218.9 us)
Sparse Core Ops, SparseCore 0:
  313.1 37.6 all-reduce.11
  357.7 266.8 all-reduce.13
